TPU v7x, 32 devices: a whole 2x2x4 slice. The times are simulated.
32 devices in a mesh: row: 4 (over x, core), col: 8 (over z, y).
Axes of the slice: x: 2, y: 2, z: 4, core: 2. Of those that a mesh axis runs over, the one named last changes fastest.
Arguments:
- item_ids: int32 [8192], P(('row', 'col')), may hold values from 0 to 63
- user_lengths: int32 [8], replicated, may hold values from 1 to 2048, 8192 in all
- catalogue: bfloat16 [64, 1024], P(('row', 'col')), may hold values from -6 to 6
- tap_lengths: int32 [1, 1024], replicated, may hold values from 64 to 256
- conv_taps: bfloat16 [1, 256, 1024], replicated, may hold values from -0.375 to 0.375
- norm_gains: float32 [1, 2, 1024], replicated, may hold values from 0.1 to 1.9
- gate_weight: bfloat16 [1, 1024, 1024], P(None, 'col'), may hold values from -0.1875 to 0.1875
- up_weight: bfloat16 [1, 1024, 1024], P(None, 'col'), may hold values from -0.1875 to 0.1875
- down_weight: bfloat16 [1, 1024, 1024], P(None, 'col'), may hold values from -0.1875 to 0.1875
Outputs:
- history_out: bfloat16 [8192, 1024], P(('row', 'col'))
Inputs may be any that keep to these rules, and one draw needn't show every extreme that they name: `user_lengths`: the 8 lengths sum to 8192.
All inputs are finite; a program needn't handle non-finite values.
Results may differ from a plain program's by a relative error of at most 0.0054.
Values may be sent and summed in bfloat16 or wider, within the bound.
No kernel may reach another device: no remote copies, remote signals or barrier semaphores. Data moves between devices by JAX's collectives and lax.ppermute only.
A program may use at most 64 MiB of HBM per device.

v0:
```python
import jax
import jax.numpy as jnp
from jax import lax
from jax.sharding import PartitionSpec as P

epsilon = 1e-06
group_taps = 32


def from_behind(block, axis, distance):
    devices = range(lax.axis_size(axis))
    route = [(i - distance, i) for i in devices if i - distance in devices]
    return lax.ppermute(block, axis, route)


def rms_norm(values, gains):
    scale = lax.rsqrt(jnp.mean(values * values, axis=-1, keepdims=True) + epsilon)
    return values * scale * gains


def token_ages(positions, user_starts):
    reached = user_starts[None, :] <= positions[:, None]
    fallback = jnp.minimum(positions, 0)[:, None]
    seg_start = jnp.max(jnp.where(reached, user_starts[None, :], fallback), axis=1)
    return positions - seg_start


def earlier_items(item_ids, wanted):
    current = item_ids
    pieces = []
    current = from_behind(current, ("row", "col"), 1)
    pieces = [current] + pieces
    return pieces[0][-wanted:]


def convolve(extended, tap_table, token_age, out_rows):
    reach = extended.shape[0] - out_rows
    groups = -(-tap_table.shape[0] // group_taps)

    def one_group(group_index, accumulated):
        for within in range(group_taps):
            lag_index = group_index * group_taps + within
            shifted = lax.dynamic_slice_in_dim(extended, reach - lag_index, out_rows, 0)
            weights = lax.dynamic_slice_in_dim(tap_table, lag_index, 1, 0)
            keep = (lag_index <= token_age)[:, None]
            accumulated = accumulated + jnp.where(keep, shifted * weights, 0.0)
        return accumulated

    blank = jnp.zeros((out_rows, extended.shape[1]), jnp.float32)
    return lax.fori_loop(0, groups, one_group, blank)


def feed_forward(hidden, gains_row, gate_rows, up_rows, down_rows):
    inner = rms_norm(hidden, gains_row).astype(jnp.bfloat16)
    columns = inner
    first_sum = jnp.dot(
        columns,
        lax.all_gather(gate_rows, "col", axis=0, tiled=True),
        preferred_element_type=jnp.float32,
    )
    second_sum = jnp.dot(
        columns,
        lax.all_gather(up_rows, "col", axis=0, tiled=True),
        preferred_element_type=jnp.float32,
    )
    activated = (jax.nn.silu(first_sum) * second_sum).astype(jnp.bfloat16)
    columns = activated
    projected = jnp.dot(
        columns,
        lax.all_gather(down_rows, "col", axis=0, tiled=True),
        preferred_element_type=jnp.float32,
    )
    return hidden + projected


def body(
    item_ids,
    user_lengths,
    catalogue,
    tap_lengths,
    conv_taps,
    norm_gains,
    gate_weight,
    up_weight,
    down_weight,
):
    row_count = item_ids.shape[0]
    reach = conv_taps.shape[1] - 1
    layer_count = conv_taps.shape[0]
    catalogue_all = lax.all_gather(catalogue, ("row", "col"), axis=0, tiled=True)
    device_index = lax.axis_index("row") * lax.axis_size("col") + lax.axis_index("col")
    first_row = device_index * row_count
    user_starts = jnp.cumsum(user_lengths) - user_lengths
    lag_column = jnp.arange(conv_taps.shape[1], dtype=jnp.int32)[:, None]
    tap_tables = conv_taps.astype(jnp.float32) * (
        lag_column[None] < tap_lengths[:, None, :]
    ).astype(jnp.float32)
    extra = reach * layer_count
    wide_ids = jnp.concatenate([earlier_items(item_ids, extra), item_ids], axis=0)
    hidden = jnp.take(catalogue_all, wide_ids, axis=0).astype(jnp.float32)
    positions = first_row - extra + jnp.arange(row_count + extra, dtype=jnp.int32)
    all_ages = token_ages(positions, user_starts)
    out_rows = row_count + reach * (layer_count - 1)
    normed = rms_norm(hidden, norm_gains[0, 0]).astype(jnp.bfloat16)
    hidden = hidden[-out_rows:] + convolve(normed, tap_tables[0], all_ages[-out_rows:], out_rows)
    hidden = feed_forward(hidden, norm_gains[0, 1], gate_weight[0], up_weight[0], down_weight[0])
    return hidden.astype(jnp.bfloat16)


def solution(mesh):
    return jax.shard_map(
        body,
        mesh=mesh,
        in_specs=(
            P(("row", "col")),
            P(),
            P(("row", "col"), None),
            P(),
            P(),
            P(),
            P(None, "col", None),
            P(None, "col", None),
            P(None, "col", None),
        ),
        out_specs=P(("row", "col"), None),
        check_vma=False,
    )
```

profile of v0, /device:TPU:2, one launch (start us, length us, event | category | flops | bytes accessed | tf_op | source)
XLA Modules:
  0.0 230.7 jit_solution(10582264455192001664)
XLA Ops:
  8.1 3.4 %collective-permute-start = (s32[256]{0:T(256)}, s32[256]{0:T(256)S(1)}, u32[]{:S(2)}, u32[]{:S(2)}) collective-permute-start(s32[256]{0:T(256)} %param.11), channel_id=1, source_target_pairs={{0,1},{1,2},{2,3},{3,4},{4,5},{5,6},{6,7},{7,8},{8,9},{9,10},{10,1... | collective-permute-start | bytes 3080 | tf_op jit(solution)/shard_map/ppermute | solution.py:13
  13.9 2.2 select_bitcast_fusion
  16.1 69.4 %all-gather.3 = bf16[32,2,1024]{2,1,0:T(2,128)(2,1)S(1)} all-gather(bf16[1,2,1024]{2,1,0:T(2,128)(2,1)S(1)} %bitcast.163), channel_id=1, replica_groups=mesh['row'=4,'col'=8] {'row','col'}, dimensions={0}, use_global_device_ids=true | all-gather | bytes 135168 | tf_op jit(solution)/shard_map/all_gather | solution.py:90
  85.9 2.1 gather_fusion
  88.8 124.7 %while.17 = (s32[]{:T(128)}, f32[256,1024]{1,0:T(8,128)S(1)}, s32[256]{0:T(256)S(1)}, bf16[511,1024]{1,0:T(8,128)(2,1)S(1)}, f32[256,1024]{1,0:T(8,128)}, /*inde...) while((s32[]{:T(128)}, f32[256,1024]{1,0:T(8,128)S(1)}, ...), condition=%wide.region_4.5_spmd.clone, body=%wide.region_3.4_spmd.clone.sunk | while | flops 33825024 | bytes 19289948 | solution.py:50
  88.9 1.5 constant_dynamic-slice_fusion.35
  90.5 1.4 constant_dynamic-slice_fusion.34
  92.3 12.3 %select_add_fusion.3 = f32[256,1024]{1,0:T(8,128)S(1)} fusion(f32[256,1024]{1,0:T(8,128)S(1)} %get-tuple-element.605, f32[1024]{0:T(1024)S(1)} %bitcast.128, bf16[511,1024]{1,0:T(8,128)(2,1)S(1)} %get-tuple-element.679, s32[]{:T(128)S(6)} %select_n.1373, f32[1024]{0:T(1024)S(1)} %bitcast.129, s32[]{:T(128)S(6)} %select_n.1374, ...), kind=kLoop, calls=%fused_computation.26.clone.1 | loop fusion | flops 33816576 | bytes 19013760 | tf_op jit(solution)/shard_map/while/body/eval_jaxpr/add | solution.py:46
  104.7 1.2 constant_dynamic-slice_fusion.35
  106.1 1.4 constant_dynamic-slice_fusion.34
  107.8 12.3 %select_add_fusion.3 = f32[256,1024]{1,0:T(8,128)S(1)} fusion(f32[256,1024]{1,0:T(8,128)S(1)} %get-tuple-element.605, f32[1024]{0:T(1024)S(1)} %bitcast.128, bf16[511,1024]{1,0:T(8,128)(2,1)S(1)} %get-tuple-element.679, s32[]{:T(128)S(6)} %select_n.1373, f32[1024]{0:T(1024)S(1)} %bitcast.129, s32[]{:T(128)S(6)} %select_n.1374, ...), kind=kLoop, calls=%fused_computation.26.clone.1 | loop fusion | flops 33816576 | bytes 19013760 | tf_op jit(solution)/shard_map/while/body/eval_jaxpr/add | solution.py:46
  120.3 1.2 constant_dynamic-slice_fusion.35
  121.6 1.4 constant_dynamic-slice_fusion.34
  123.4 12.3 %select_add_fusion.3 = f32[256,1024]{1,0:T(8,128)S(1)} fusion(f32[256,1024]{1,0:T(8,128)S(1)} %get-tuple-element.605, f32[1024]{0:T(1024)S(1)} %bitcast.128, bf16[511,1024]{1,0:T(8,128)(2,1)S(1)} %get-tuple-element.679, s32[]{:T(128)S(6)} %select_n.1373, f32[1024]{0:T(1024)S(1)} %bitcast.129, s32[]{:T(128)S(6)} %select_n.1374, ...), kind=kLoop, calls=%fused_computation.26.clone.1 | loop fusion | flops 33816576 | bytes 19013760 | tf_op jit(solution)/shard_map/while/body/eval_jaxpr/add | solution.py:46
  135.8 1.2 constant_dynamic-slice_fusion.35
  137.2 1.4 constant_dynamic-slice_fusion.34
  138.9 12.3 %select_add_fusion.3 = f32[256,1024]{1,0:T(8,128)S(1)} fusion(f32[256,1024]{1,0:T(8,128)S(1)} %get-tuple-element.605, f32[1024]{0:T(1024)S(1)} %bitcast.128, bf16[511,1024]{1,0:T(8,128)(2,1)S(1)} %get-tuple-element.679, s32[]{:T(128)S(6)} %select_n.1373, f32[1024]{0:T(1024)S(1)} %bitcast.129, s32[]{:T(128)S(6)} %select_n.1374, ...), kind=kLoop, calls=%fused_computation.26.clone.1 | loop fusion | flops 33816576 | bytes 19013760 | tf_op jit(solution)/shard_map/while/body/eval_jaxpr/add | solution.py:46
  151.4 1.2 constant_dynamic-slice_fusion.35
  152.7 1.4 constant_dynamic-slice_fusion.34
  154.5 12.3 %select_add_fusion.3 = f32[256,1024]{1,0:T(8,128)S(1)} fusion(f32[256,1024]{1,0:T(8,128)S(1)} %get-tuple-element.605, f32[1024]{0:T(1024)S(1)} %bitcast.128, bf16[511,1024]{1,0:T(8,128)(2,1)S(1)} %get-tuple-element.679, s32[]{:T(128)S(6)} %select_n.1373, f32[1024]{0:T(1024)S(1)} %bitcast.129, s32[]{:T(128)S(6)} %select_n.1374, ...), kind=kLoop, calls=%fused_computation.26.clone.1 | loop fusion | flops 33816576 | bytes 19013760 | tf_op jit(solution)/shard_map/while/body/eval_jaxpr/add | solution.py:46
  166.9 1.2 constant_dynamic-slice_fusion.35
  168.3 1.4 constant_dynamic-slice_fusion.34
  170.0 12.3 %select_add_fusion.3 = f32[256,1024]{1,0:T(8,128)S(1)} fusion(f32[256,1024]{1,0:T(8,128)S(1)} %get-tuple-element.605, f32[1024]{0:T(1024)S(1)} %bitcast.128, bf16[511,1024]{1,0:T(8,128)(2,1)S(1)} %get-tuple-element.679, s32[]{:T(128)S(6)} %select_n.1373, f32[1024]{0:T(1024)S(1)} %bitcast.129, s32[]{:T(128)S(6)} %select_n.1374, ...), kind=kLoop, calls=%fused_computation.26.clone.1 | loop fusion | flops 33816576 | bytes 19013760 | tf_op jit(solution)/shard_map/while/body/eval_jaxpr/add | solution.py:46
  182.5 1.2 constant_dynamic-slice_fusion.35
  183.8 1.4 constant_dynamic-slice_fusion.34
  185.6 12.3 %select_add_fusion.3 = f32[256,1024]{1,0:T(8,128)S(1)} fusion(f32[256,1024]{1,0:T(8,128)S(1)} %get-tuple-element.605, f32[1024]{0:T(1024)S(1)} %bitcast.128, bf16[511,1024]{1,0:T(8,128)(2,1)S(1)} %get-tuple-element.679, s32[]{:T(128)S(6)} %select_n.1373, f32[1024]{0:T(1024)S(1)} %bitcast.129, s32[]{:T(128)S(6)} %select_n.1374, ...), kind=kLoop, calls=%fused_computation.26.clone.1 | loop fusion | flops 33816576 | bytes 19013760 | tf_op jit(solution)/shard_map/while/body/eval_jaxpr/add | solution.py:46
  198.0 1.2 constant_dynamic-slice_fusion.35
  199.4 1.4 constant_dynamic-slice_fusion.34
  201.2 12.3 %select_add_fusion.3 = f32[256,1024]{1,0:T(8,128)S(1)} fusion(f32[256,1024]{1,0:T(8,128)S(1)} %get-tuple-element.605, f32[1024]{0:T(1024)S(1)} %bitcast.128, bf16[511,1024]{1,0:T(8,128)(2,1)S(1)} %get-tuple-element.679, s32[]{:T(128)S(6)} %select_n.1373, f32[1024]{0:T(1024)S(1)} %bitcast.129, s32[]{:T(128)S(6)} %select_n.1374, ...), kind=kLoop, calls=%fused_computation.26.clone.1 | loop fusion | flops 33816576 | bytes 19013760 | tf_op jit(solution)/shard_map/while/body/eval_jaxpr/add | solution.py:46
  213.7 1.3 copy-done
  215.4 3.9 %fusion.28 = f32[256,1024]{1,0:T(8,128)} fusion(bf16[1,1024,1024]{2,1,0:T(8,128)(2,1)} %all-gather.8.cloned.1.call-done, f32[1024]{0:T(1024)S(1)} %bitcast.165, f32[256]{0:T(256)S(1)} %add_rsqrt_fusion.1, f32[256,1024]{1,0:T(8,128)S(1)} %get-tuple-element.276, f32[511,1024]{1,0:T(8,128)} %copy-done), kind=kOutput, calls=%fused_computation.95 | convolution fusion | flops 537919488 | bytes 5248000 | tf_op jit(solution)/shard_map/dot_general | solution.py:56
  219.3 4.9 %fusion.36 = bf16[256,1024]{1,0:T(8,128)(2,1)} fusion(bf16[1,1024,1024]{2,1,0:T(8,128)(2,1)} %all-gather.12.cloned.1.call-done, bf16[1,1024,1024]{2,1,0:T(8,128)(2,1)} %all-gather.10.cloned.1.call-done, f32[256,1024]{1,0:T(8,128)} %fusion.28, f32[1024]{0:T(1024)S(1)} %bitcast.166, f32[256]{0:T(256)S(1)} %add_rsqrt_fusion.1, ...), kind=kOutput, calls=%fused_computation.101 | convolution fusion | flops 1077149696 | bytes 9966592 | tf_op jit(solution)/shard_map/dot_general | solution.py:68
  (52 shorter events, 6.1 us)
Async XLA Ops:
  6.5 79.2 %copy-start.3 = (s32[256]{0:T(256)S(1)}, s32[256]{0:T(256)}, u32[]{:S(2)}) copy-start(s32[256]{0:T(256)} %param.11) | copy-start | bytes 3076
  6.5 9.6 %copy-start.2 = (bf16[2,1024]{1,0:T(2,128)(2,1)S(1)}, bf16[2,1024]{1,0:T(2,128)(2,1)}, u32[]{:S(2)}) copy-start(bf16[2,1024]{1,0:T(2,128)(2,1)} %param.13) | copy-start | bytes 12292
  6.5 208.8 %all-gather.8.cloned.1.call-start = ((), (), s32[]{:S(2)}) async-start(), calls=%async_computation | async-start | bytes 2359296 | tf_op jit(solution)/shard_map/all_gather | solution.py:58
  7.3 212.0 %all-gather.10.cloned.1.call-start = ((), (), s32[]{:S(2)}) async-start(), calls=%async_computation.1 | async-start | bytes 2359296 | tf_op jit(solution)/shard_map/all_gather | solution.py:63
  8.0 211.3 %all-gather.12.cloned.1.call-start = ((), (), s32[]{:S(2)}) async-start(), calls=%async_computation.2 | async-start | bytes 2359296 | tf_op jit(solution)/shard_map/all_gather | solution.py:70
  8.1 77.6 %collective-permute-start = (s32[256]{0:T(256)}, s32[256]{0:T(256)S(1)}, u32[]{:S(2)}, u32[]{:S(2)}) collective-permute-start(s32[256]{0:T(256)} %param.11), channel_id=1, source_target_pairs={{0,1},{1,2},{2,3},{3,4},{4,5},{5,6},{6,7},{7,8},{8,9},{9,10},{10,1... | collective-permute-start | bytes 3080 | tf_op jit(solution)/shard_map/ppermute | solution.py:13
  213.7 1.4 copy-start
  215.4 3.9 %copy-start.1 = (f32[511,1024]{1,0:T(8,128)S(1)}, f32[511,1024]{1,0:T(8,128)}, u32[]{:S(2)}) copy-start(f32[511,1024]{1,0:T(8,128)} %copy-done) | copy-start | bytes 6279172
Sparse Core Ops, SparseCore 0:
  9.5 50.3 all-gather.7
  62.0 48.4 all-gather.9
  112.6 47.6 all-gather.11
where the time goes:
time: 233 us; the launch traced here: 231 us
  other arithmetic  104 us (45%)
  blocking collectives  69.4 us (30%)
  local copies, waits for them, and re-layouts  25.8 us (11%)
  between operations  13.2 us (6%)
  matrix products  8.77 us (4%)
  loops' own time  4.23 us (2%)
  starting transfers between devices  3.51 us (2%)
    add x8, other arithmetic, one_group(): accumulated = accumulated + jnp.where(keep, shifted * weights, 0.0)  98.5 us
    all_gather x1, blocking collectives, body(): lax.all_gather(catalogue, ('row', 'col'), axis=0, tiled=True)  69.4 us
    dynamic_slice x16, local copies, waits for them, and re-layouts, one_group(): weights = lax.dynamic_slice_in_dim(tap_table, lag_index, 1, 0)  21.4 us
    dot_general x1, matrix products, feed_forward(): jnp.dot(columns, lax.all_gather(down_rows, 'col', axis=0, tiled=True), pr...  4.87 us
  transfers between devices with their start and end apart: 4, of which 0 were waited for; matrix products, arithmetic and copies ran while one was open for 57% of the time, Pallas kernels for 0%

commit v1 on v0

--- a/solution.py
+++ b/solution.py
@@ -87,7 +87,12 @@
     row_count = item_ids.shape[0]
     reach = conv_taps.shape[1] - 1
     layer_count = conv_taps.shape[0]
-    catalogue_all = lax.all_gather(catalogue, ("row", "col"), axis=0, tiled=True)
+    catalogue_all = jnp.concatenate(
+        lax.all_to_all(
+            jnp.stack([catalogue] * lax.axis_size(("row", "col"))), ("row", "col"), 0, 0
+        ),
+        axis=0,
+    )
     device_index = lax.axis_index("row") * lax.axis_size("col") + lax.axis_index("col")
     first_row = device_index * row_count
     user_starts = jnp.cumsum(user_lengths) - user_lengths

time: 233 us -> 177 us (0.76)
  the two profiles are of different devices: /device:TPU:2 before, /device:TPU:0 now
where the time goes in v1:
time: 177 us; the launch traced here: 175 us
  other arithmetic  104 us (59%)
  local copies, waits for them, and re-layouts  29.5 us (17%)
  between operations  13.2 us (7%)
  starting transfers between devices  9.88 us (6%)
  matrix products  8.79 us (5%)
  waiting for transfers between devices  4.83 us (3%)
  loops' own time  4.23 us (2%)
    add x8, other arithmetic, one_group(): accumulated = accumulated + jnp.where(keep, shifted * weights, 0.0)  98.5 us
    dynamic_slice x16, local copies, waits for them, and re-layouts, one_group(): weights = lax.dynamic_slice_in_dim(tap_table, lag_index, 1, 0)  23.7 us
    ppermute x1, starting transfers between devices, from_behind(): return lax.ppermute(block, axis, route)  4.9 us
    all_to_all x1, starting transfers between devices, body(): lax.all_to_all(jnp.stack([catalogue] * lax.axis_size(('row', 'col'))), ('...  4.9 us
    dot_general x1, matrix products, feed_forward(): jnp.dot(columns, lax.all_gather(down_rows, 'col', axis=0, tiled=True), pr...  4.88 us
    another operation x1, loops' own time, convolve(): return lax.fori_loop(0, groups, one_group, blank)  4.23 us
    dot_general x1, matrix products, feed_forward(): jnp.dot(columns, lax.all_gather(gate_rows, 'col', axis=0, tiled=True), pr...  3.91 us
  transfers between devices with their start and end apart: 5, of which 1 were waited for; matrix products, arithmetic and copies ran while one was open for 78% of the time, Pallas kernels for 0%

profile of v1, /device:TPU:0, one launch (start us, length us, event | category | flops | bytes accessed | tf_op | source)
XLA Modules:
  0.0 174.7 jit_solution(3194262761606815539)
XLA Ops:
  8.0 4.9 %collective-permute-start = (s32[256]{0:T(256)}, s32[256]{0:T(256)S(1)}, u32[]{:S(2)}, u32[]{:S(2)}) collective-permute-start(s32[256]{0:T(256)} %param.11), channel_id=1, source_target_pairs={{0,1},{1,2},{2,3},{3,4},{4,5},{5,6},{6,7},{7,8},{8,9},{9,10},{10,1... | collective-permute-start | bytes 3080 | tf_op jit(solution)/shard_map/ppermute | solution.py:13
  12.9 1.4 stack.2
  14.3 4.9 %all-to-all-start = ((bf16[32,2,1024]{2,1,0:T(2,128)(2,1)}), bf16[32,2,1024]{2,1,0:T(2,128)(2,1)S(1)}, u32[]{:S(2)}, u32[]{:S(2)}) async-start(bf16[32,2,1024]{2,1,0:T(2,128)(2,1)} %stack.2), calls=%async_computation | async-start | bytes 262144 | tf_op jit(solution)/shard_map/all_to_all | solution.py:91
  22.3 2.2 %select_bitcast_fusion = f32[256,1024]{1,0:T(8,128)} fusion(bf16[1,256,1024]{2,1,0:T(8,128)(2,1)} %param.15, s32[1024]{0:T(1024)} %bitcast.161), kind=kLoop, calls=%fused_computation.106 | loop fusion | flops 786432 | bytes 1576960 | tf_op jit(solution)/shard_map/squeeze | solution.py:110
  24.9 2.7 %all-to-all-done = bf16[32,2,1024]{2,1,0:T(2,128)(2,1)S(1)} async-done(((bf16[32,2,1024]{2,1,0:T(2,128)(2,1)}), bf16[32,2,1024]{2,1,0:T(2,128)(2,1)S(1)}, u32[]{:S(2)}, u32[]{:S(2)}) %all-to-all-start) | async-done | bytes 131104 | tf_op jit(solution)/shard_map/all_to_all | solution.py:91
  27.6 2.1 %gather_fusion = bf16[511,1024]{1,0:T(8,128)(2,1)S(1)} fusion(bf16[64,1024]{1,0:T(8,128)(2,1)S(1)} %reshape.380, s32[1024]{0:T(1024)S(1)} %pad_clamp_fusion), kind=kCustom, calls=%fused_computation | custom fusion | bytes 2095100 | tf_op jit(solution)/shard_map/jit(_take)/gather | solution.py:105
  30.6 126.9 %while.17 = (s32[]{:T(128)}, f32[256,1024]{1,0:T(8,128)S(1)}, s32[256]{0:T(256)S(1)}, bf16[511,1024]{1,0:T(8,128)(2,1)S(1)}, f32[256,1024]{1,0:T(8,128)}, /*inde...) while((s32[]{:T(128)}, f32[256,1024]{1,0:T(8,128)S(1)}, ...), condition=%wide.region_4.5_spmd.clone, body=%wide.region_3.4_spmd.clone.sunk | while | flops 33825024 | bytes 19289948 | solution.py:50
  30.7 1.5 constant_dynamic-slice_fusion.35
  32.3 1.6 constant_dynamic-slice_fusion.34
  34.2 12.3 %select_add_fusion.3 = f32[256,1024]{1,0:T(8,128)S(1)} fusion(f32[256,1024]{1,0:T(8,128)S(1)} %get-tuple-element.605, f32[1024]{0:T(1024)S(1)} %bitcast.127, bf16[511,1024]{1,0:T(8,128)(2,1)S(1)} %get-tuple-element.679, s32[]{:T(128)S(6)} %select_n.1373, f32[1024]{0:T(1024)S(1)} %bitcast.128, s32[]{:T(128)S(6)} %select_n.1374, ...), kind=kLoop, calls=%fused_computation.26.clone.1 | loop fusion | flops 33816576 | bytes 19013760 | tf_op jit(solution)/shard_map/while/body/eval_jaxpr/add | solution.py:46
  46.7 1.4 constant_dynamic-slice_fusion.35
  48.2 1.6 constant_dynamic-slice_fusion.34
  50.2 12.3 %select_add_fusion.3 = f32[256,1024]{1,0:T(8,128)S(1)} fusion(f32[256,1024]{1,0:T(8,128)S(1)} %get-tuple-element.605, f32[1024]{0:T(1024)S(1)} %bitcast.127, bf16[511,1024]{1,0:T(8,128)(2,1)S(1)} %get-tuple-element.679, s32[]{:T(128)S(6)} %select_n.1373, f32[1024]{0:T(1024)S(1)} %bitcast.128, s32[]{:T(128)S(6)} %select_n.1374, ...), kind=kLoop, calls=%fused_computation.26.clone.1 | loop fusion | flops 33816576 | bytes 19013760 | tf_op jit(solution)/shard_map/while/body/eval_jaxpr/add | solution.py:46
  62.6 1.4 constant_dynamic-slice_fusion.35
  64.2 1.4 constant_dynamic-slice_fusion.34
  66.0 12.3 %select_add_fusion.3 = f32[256,1024]{1,0:T(8,128)S(1)} fusion(f32[256,1024]{1,0:T(8,128)S(1)} %get-tuple-element.605, f32[1024]{0:T(1024)S(1)} %bitcast.127, bf16[511,1024]{1,0:T(8,128)(2,1)S(1)} %get-tuple-element.679, s32[]{:T(128)S(6)} %select_n.1373, f32[1024]{0:T(1024)S(1)} %bitcast.128, s32[]{:T(128)S(6)} %select_n.1374, ...), kind=kLoop, calls=%fused_computation.26.clone.1 | loop fusion | flops 33816576 | bytes 19013760 | tf_op jit(solution)/shard_map/while/body/eval_jaxpr/add | solution.py:46
  78.4 1.5 constant_dynamic-slice_fusion.35
  80.0 1.7 constant_dynamic-slice_fusion.34
  82.1 12.3 %select_add_fusion.3 = f32[256,1024]{1,0:T(8,128)S(1)} fusion(f32[256,1024]{1,0:T(8,128)S(1)} %get-tuple-element.605, f32[1024]{0:T(1024)S(1)} %bitcast.127, bf16[511,1024]{1,0:T(8,128)(2,1)S(1)} %get-tuple-element.679, s32[]{:T(128)S(6)} %select_n.1373, f32[1024]{0:T(1024)S(1)} %bitcast.128, s32[]{:T(128)S(6)} %select_n.1374, ...), kind=kLoop, calls=%fused_computation.26.clone.1 | loop fusion | flops 33816576 | bytes 19013760 | tf_op jit(solution)/shard_map/while/body/eval_jaxpr/add | solution.py:46
  95.9 1.6 constant_dynamic-slice_fusion.34
  97.8 12.3 %select_add_fusion.3 = f32[256,1024]{1,0:T(8,128)S(1)} fusion(f32[256,1024]{1,0:T(8,128)S(1)} %get-tuple-element.605, f32[1024]{0:T(1024)S(1)} %bitcast.127, bf16[511,1024]{1,0:T(8,128)(2,1)S(1)} %get-tuple-element.679, s32[]{:T(128)S(6)} %select_n.1373, f32[1024]{0:T(1024)S(1)} %bitcast.128, s32[]{:T(128)S(6)} %select_n.1374, ...), kind=kLoop, calls=%fused_computation.26.clone.1 | loop fusion | flops 33816576 | bytes 19013760 | tf_op jit(solution)/shard_map/while/body/eval_jaxpr/add | solution.py:46
  111.7 1.7 constant_dynamic-slice_fusion.34
  113.7 12.3 %select_add_fusion.3 = f32[256,1024]{1,0:T(8,128)S(1)} fusion(f32[256,1024]{1,0:T(8,128)S(1)} %get-tuple-element.605, f32[1024]{0:T(1024)S(1)} %bitcast.127, bf16[511,1024]{1,0:T(8,128)(2,1)S(1)} %get-tuple-element.679, s32[]{:T(128)S(6)} %select_n.1373, f32[1024]{0:T(1024)S(1)} %bitcast.128, s32[]{:T(128)S(6)} %select_n.1374, ...), kind=kLoop, calls=%fused_computation.26.clone.1 | loop fusion | flops 33816576 | bytes 19013760 | tf_op jit(solution)/shard_map/while/body/eval_jaxpr/add | solution.py:46
  126.1 1.3 constant_dynamic-slice_fusion.35
  127.5 1.4 constant_dynamic-slice_fusion.34
  129.3 12.3 %select_add_fusion.3 = f32[256,1024]{1,0:T(8,128)S(1)} fusion(f32[256,1024]{1,0:T(8,128)S(1)} %get-tuple-element.605, f32[1024]{0:T(1024)S(1)} %bitcast.127, bf16[511,1024]{1,0:T(8,128)(2,1)S(1)} %get-tuple-element.679, s32[]{:T(128)S(6)} %select_n.1373, f32[1024]{0:T(1024)S(1)} %bitcast.128, s32[]{:T(128)S(6)} %select_n.1374, ...), kind=kLoop, calls=%fused_computation.26.clone.1 | loop fusion | flops 33816576 | bytes 19013760 | tf_op jit(solution)/shard_map/while/body/eval_jaxpr/add | solution.py:46
  141.7 1.3 constant_dynamic-slice_fusion.35
  143.2 1.6 constant_dynamic-slice_fusion.34
  145.2 12.3 %select_add_fusion.3 = f32[256,1024]{1,0:T(8,128)S(1)} fusion(f32[256,1024]{1,0:T(8,128)S(1)} %get-tuple-element.605, f32[1024]{0:T(1024)S(1)} %bitcast.127, bf16[511,1024]{1,0:T(8,128)(2,1)S(1)} %get-tuple-element.679, s32[]{:T(128)S(6)} %select_n.1373, f32[1024]{0:T(1024)S(1)} %bitcast.128, s32[]{:T(128)S(6)} %select_n.1374, ...), kind=kLoop, calls=%fused_computation.26.clone.1 | loop fusion | flops 33816576 | bytes 19013760 | tf_op jit(solution)/shard_map/while/body/eval_jaxpr/add | solution.py:46
  157.7 1.3 copy-done
  159.4 3.9 %fusion.28 = f32[256,1024]{1,0:T(8,128)} fusion(bf16[1,1024,1024]{2,1,0:T(8,128)(2,1)} %all-gather.7.cloned.1.call-done, f32[1024]{0:T(1024)S(1)} %bitcast.163, f32[256]{0:T(256)S(1)} %add_rsqrt_fusion.1, f32[256,1024]{1,0:T(8,128)S(1)} %get-tuple-element.276, f32[511,1024]{1,0:T(8,128)} %copy-done), kind=kOutput, calls=%fused_computation.95 | convolution fusion | flops 537919488 | bytes 5248000 | tf_op jit(solution)/shard_map/dot_general | solution.py:56
  163.3 4.9 %fusion.36 = bf16[256,1024]{1,0:T(8,128)(2,1)} fusion(bf16[1,1024,1024]{2,1,0:T(8,128)(2,1)} %all-gather.11.cloned.1.call-done, bf16[1,1024,1024]{2,1,0:T(8,128)(2,1)} %all-gather.9.cloned.1.call-done, f32[256,1024]{1,0:T(8,128)} %fusion.28, f32[1024]{0:T(1024)S(1)} %bitcast.164, f32[256]{0:T(256)S(1)} %add_rsqrt_fusion.1, ...), kind=kOutput, calls=%fused_computation.101 | convolution fusion | flops 1077149696 | bytes 9966592 | tf_op jit(solution)/shard_map/dot_general | solution.py:68
  (52 shorter events, 9.4 us)
Async XLA Ops:
  6.5 18.2 %copy-start.2 = (s32[256]{0:T(256)S(1)}, s32[256]{0:T(256)}, u32[]{:S(2)}) copy-start(s32[256]{0:T(256)} %param.11) | copy-start | bytes 3076
  6.5 152.8 %all-gather.7.cloned.1.call-start = ((), (), s32[]{:S(2)}) async-start(), calls=%async_computation.1 | async-start | bytes 2359296 | tf_op jit(solution)/shard_map/all_gather | solution.py:58
  7.3 156.0 %all-gather.11.cloned.1.call-start = ((), (), s32[]{:S(2)}) async-start(), calls=%async_computation.3 | async-start | bytes 2359296 | tf_op jit(solution)/shard_map/all_gather | solution.py:70
  8.0 16.6 %collective-permute-start = (s32[256]{0:T(256)}, s32[256]{0:T(256)S(1)}, u32[]{:S(2)}, u32[]{:S(2)}) collective-permute-start(s32[256]{0:T(256)} %param.11), channel_id=1, source_target_pairs={{0,1},{1,2},{2,3},{3,4},{4,5},{5,6},{6,7},{7,8},{8,9},{9,10},{10,1... | collective-permute-start | bytes 3080 | tf_op jit(solution)/shard_map/ppermute | solution.py:13
  14.3 13.3 %all-to-all-start = ((bf16[32,2,1024]{2,1,0:T(2,128)(2,1)}), bf16[32,2,1024]{2,1,0:T(2,128)(2,1)S(1)}, u32[]{:S(2)}, u32[]{:S(2)}) async-start(bf16[32,2,1024]{2,1,0:T(2,128)(2,1)} %stack.2), calls=%async_computation | async-start | bytes 262144 | tf_op jit(solution)/shard_map/all_to_all | solution.py:91
  19.2 144.1 %all-gather.9.cloned.1.call-start = ((), (), s32[]{:S(2)}) async-start(), calls=%async_computation.2 | async-start | bytes 2359296 | tf_op jit(solution)/shard_map/all_gather | solution.py:63
  157.7 1.3 copy-start
  159.4 3.9 %copy-start.1 = (f32[511,1024]{1,0:T(8,128)S(1)}, f32[511,1024]{1,0:T(8,128)}, u32[]{:S(2)}) copy-start(f32[511,1024]{1,0:T(8,128)} %copy-done) | copy-start | bytes 6279172
Sparse Core Ops, SparseCore 0:
  9.5 53.3 all-gather.6
  65.0 47.6 all-gather.10
  114.8 47.5 all-gather.8
